TPU v7x, 128 devices: a whole 4x4x4 slice. The times are simulated.
128 devices in a mesh: gx: 8 (over y, core), gy: 8 (over x, z_hi), ga: 2 (over z_lo).
Axes of the slice: x: 4, y: 4, z: 4 (z_hi: 2, z_lo: 2; z = z_hi * 2 + z_lo), core: 2. Of those that a mesh axis runs over, the one named last changes fastest.
Arguments:
- offsets: float32 [3, 16, 16, 32, 128], P(None, 'gx', 'gy', 'ga'), may hold values from 0 to 1
- charge: float32 [16, 16, 32, 128], P('gx', 'gy', 'ga'), may hold values from -3 to 3
- counts: int32 [16, 16, 32], P('gx', 'gy', 'ga'), may hold values from 8 to 128, as said below
- partners: int32 [16, 16, 32, 128], P('gx', 'gy', 'ga'), may hold values from 0 to 127
Outputs:
- short_force: float32 [3, 16, 16, 32, 128], P(None, 'gx', 'gy', 'ga')
- long_force: float32 [3, 16, 16, 32, 128], P(None, 'gx', 'gy', 'ga')
Inputs may be any that keep to these rules, and one draw needn't show every extreme that they name: `counts`: each cell holds at least 8 beads and at most 128; some cell holds exactly 128.
All inputs are finite; a program needn't handle non-finite values.
Results may differ from a plain program's by a relative error of at most 0.0003.
Values sent between devices are 32-bit elements; how exact they have to be, the bound alone decides.
No kernel may reach another device: no remote copies, remote signals or barrier semaphores. Data moves between devices by JAX's collectives and lax.ppermute only.
A program may use at most 192 MiB of HBM per device.

v0:
```python
import jax
import jax.numpy as jnp
from jax import lax
from jax.sharding import PartitionSpec as P

highest = lax.Precision.HIGHEST
cutoff_sq = 64.0
soften_sq = 1.0
bond_spring = 0.1
fine_scale = 4.0
coarse_scale = 2.0
fine_spread = 2.5
coarse_spread = 6.0


def padded_2(value, sides, width):
    for axis, dim in sides:
        size, length = (lax.axis_size(axis), value.shape[dim])
        up = [(i, (i + 1) % size) for i in range(size - 1)]
        down = [(j, i) for i, j in up]
        last = lax.slice_in_dim(value, length - width, length, axis=dim)
        initial = lax.slice_in_dim(value, 0, width, axis=dim)
        before = lax.ppermute(last, axis, up)
        after = lax.ppermute(initial, axis, down)
        value = jnp.concatenate([before, value, after], axis=dim)
    return value


def spline(shifted):
    magnitude = jnp.abs(shifted)
    margin = jnp.maximum(1.5 - magnitude, 0.0)
    return jnp.where(magnitude < 0.5, 0.75 - shifted * shifted, 0.5 * margin * margin)


def spline_slope(shifted):
    magnitude = jnp.abs(shifted)
    margin = jnp.maximum(1.5 - magnitude, 0.0)
    return jnp.where(magnitude < 0.5, -2.0 * shifted, jnp.where(shifted > 0.0, -margin, margin))


def patch_weights(offset):
    points = jnp.arange(11).astype(jnp.float32)
    shifted = 8.0 * offset[..., None] + 1.0 - points
    return (spline(shifted), spline_slope(shifted))


def charge_patches(weighted, offsets):
    weight_x, _ = patch_weights(offsets[0])
    weight_y, _ = patch_weights(offsets[1])
    weight_z, _ = patch_weights(offsets[2])
    plane_part = weighted[..., None, None] * weight_x[..., :, None] * weight_y[..., None, :]
    flattened = plane_part.reshape(plane_part.shape[:-2] + (121,))
    joined = jnp.einsum("...sp,...sc->...pc", flattened, weight_z, precision=highest)
    return joined.reshape(joined.shape[:-2] + (11, 11, 11))


def assemble(values, where_axis):
    cell_count = values.shape[where_axis]
    inner_part = lax.slice_in_dim(values, 0, 8, axis=where_axis + 1)
    overflow = lax.slice_in_dim(values, 8, 11, axis=where_axis + 1)
    inner_pad = [(0, 0)] * values.ndim
    inner_pad[where_axis] = (0, 1)
    over_pad = [(0, 0)] * values.ndim
    over_pad[where_axis] = (1, 0)
    over_pad[where_axis + 1] = (0, 5)
    merged = jnp.pad(inner_part, inner_pad) + jnp.pad(overflow, over_pad)
    new_shape = values.shape[:where_axis] + (8 * (cell_count + 1),) + values.shape[where_axis + 2 :]
    return merged.reshape(new_shape)


def cut_patches(values, where_axis):
    cell_count = (values.shape[where_axis] - 4) // 8
    split_shape = values.shape[:where_axis] + (cell_count, 8) + values.shape[where_axis + 1 :]
    head_part = lax.slice_in_dim(values, 1, 8 * cell_count + 1, axis=where_axis).reshape(
        split_shape
    )
    widths = [(0, 0)] * values.ndim
    widths[where_axis] = (0, 5)
    padded = jnp.pad(values, widths)
    tail_part = lax.slice_in_dim(padded, 9, 8 * cell_count + 9, axis=where_axis).reshape(
        split_shape
    )
    tail_part = lax.slice_in_dim(tail_part, 0, 3, axis=where_axis + 1)
    return jnp.concatenate([head_part, tail_part], axis=where_axis + 1)


def kernel_band(in_length, spread):
    row_index = jnp.arange(in_length)[:, None]
    column_index = jnp.arange(in_length - 16)[None, :]
    distance = row_index - column_index - 8
    gap = distance.astype(jnp.float32)
    return jnp.where(jnp.abs(distance) <= 8, jnp.exp(-gap * gap / (2.0 * spread * spread)), 0.0)


def along_axis(values, matrix, where_axis):
    contracted = jnp.tensordot(values, matrix, axes=([where_axis], [0]), precision=highest)
    return jnp.moveaxis(contracted, -1, where_axis)


def convolve(values, spread, strength):
    for where_axis in range(3):
        values = along_axis(values, kernel_band(values.shape[where_axis], spread), where_axis)
    return strength * values


def grid_map(fine_length, coarse_length, fine_start, coarse_start):
    fine_index = jnp.arange(fine_length)[:, None] + fine_start
    coarse_index = jnp.arange(coarse_length)[None, :] + coarse_start
    gap = fine_index - 2 * coarse_index
    return jnp.where(gap == 0, 1.0, jnp.where(jnp.abs(gap) == 1, 0.5, 0.0)).astype(jnp.float32)


def cell_positions(offsets, first_cell):
    coordinates = []
    for dimension in range(3):
        cell_count = offsets.shape[dimension + 1]
        cell_index = jnp.arange(cell_count).astype(jnp.float32) + first_cell
        broadcast_shape = [1, 1, 1, 1]
        broadcast_shape[dimension] = cell_count
        coordinates.append((cell_index.reshape(broadcast_shape) + offsets[dimension]) * 8.0)
    return jnp.stack(coordinates)


def pair_sum(own_pos, own_charge, near_pos, near_charge):
    separation = own_pos[..., :, None] - near_pos[..., None, :]
    distance_sq = jnp.sum(separation * separation, axis=0)
    reach_left = jnp.maximum(1.0 - distance_sq / cutoff_sq, 0.0)
    strength = (
        reach_left * reach_left * reach_left / (distance_sq + soften_sq) * near_charge[..., None, :]
    )
    return own_charge * jnp.sum(separation * strength, axis=-1)


def bond_force(positions, in_use, partners):
    slot_ids = jnp.arange(positions.shape[-1])
    picker = (partners[..., :, None] == slot_ids).astype(jnp.float32)
    partner_pos = jnp.einsum("...sp,d...p->d...s", picker, positions, precision=highest)
    partner_use = jnp.einsum("...sp,...p->...s", picker, in_use, precision=highest)
    return -bond_spring * (positions - partner_pos) * (in_use * partner_use)


def grid_force(patches, weighted, offsets):
    weight_x, slope_x = patch_weights(offsets[0])
    weight_y, slope_y = patch_weights(offsets[1])
    weight_z, slope_z = patch_weights(offsets[2])
    flattened = patches.reshape(patches.shape[:-3] + (121, 11))
    level_part = jnp.einsum("...pc,...sc->...sp", flattened, weight_z, precision=highest)
    rising = jnp.einsum("...pc,...sc->...sp", flattened, slope_z, precision=highest)
    level_part = level_part.reshape(level_part.shape[:-1] + (11, 11))
    rising = rising.reshape(rising.shape[:-1] + (11, 11))
    force_x = jnp.sum(slope_x[..., :, None] * weight_y[..., None, :] * level_part, axis=(-2, -1))
    force_y = jnp.sum(weight_x[..., :, None] * slope_y[..., None, :] * level_part, axis=(-2, -1))
    force_z = jnp.sum(weight_x[..., :, None] * weight_y[..., None, :] * rising, axis=(-2, -1))
    return -weighted * jnp.stack([force_x, force_y, force_z])


def inside_grid(fine_length, first_point, device_count):
    coordinate = jnp.arange(fine_length + 4) - 2 + first_point
    return ((coordinate >= 0) & (coordinate < fine_length * device_count)).astype(jnp.float32)


def per_device(offsets, charge, counts, partners):
    slot_count = charge.shape[-1]
    cells_x, cells_y, cells_z = charge.shape[:3]
    in_use = (jnp.arange(slot_count) < counts[..., None]).astype(jnp.float32)
    weighted = charge * in_use
    packed = jnp.concatenate([offsets, weighted[None]], axis=0)
    grown_tiles = padded_2(packed, (("gx", 1), ("gy", 2), ("ga", 3)), 1)
    grown_offsets = grown_tiles[:3]
    grown_charge = grown_tiles[3]
    grown_pos = cell_positions(grown_offsets, -1.0)
    positions = grown_pos[:, 1 : cells_x + 1, 1 : cells_y + 1, 1 : cells_z + 1]
    block_cells = 8

    def pair_block(start):
        pos_part = lax.dynamic_slice_in_dim(grown_pos, start, block_cells + 2, axis=3)
        charge_part = lax.dynamic_slice_in_dim(grown_charge, start, block_cells + 2, axis=2)
        own_pos = pos_part[:, 1 : cells_x + 1, 1 : cells_y + 1, 1 : block_cells + 1]
        own_charge = charge_part[1 : cells_x + 1, 1 : cells_y + 1, 1 : block_cells + 1]
        near_pos = jnp.concatenate(
            [
                pos_part[
                    :,
                    step_x : step_x + cells_x,
                    step_y : step_y + cells_y,
                    step_z : step_z + block_cells,
                ]
                for step_x in range(3)
                for step_y in range(3)
                for step_z in range(3)
            ],
            axis=-1,
        )
        near_charge = jnp.concatenate(
            [
                charge_part[
                    step_x : step_x + cells_x,
                    step_y : step_y + cells_y,
                    step_z : step_z + block_cells,
                ]
                for step_x in range(3)
                for step_y in range(3)
                for step_z in range(3)
            ],
            axis=-1,
        )
        return pair_sum(own_pos, own_charge, near_pos, near_charge)

    starts = jnp.arange(cells_z // block_cells) * block_cells
    block_forces = lax.map(pair_block, starts)
    pair_part = jnp.moveaxis(block_forces, 0, 3).reshape(positions.shape)
    short_force = pair_part + bond_force(positions, in_use, partners)
    patches = charge_patches(grown_charge, grown_offsets)
    spread_grid = jnp.transpose(patches, (0, 3, 1, 4, 2, 5))
    for where_axis in range(3):
        spread_grid = assemble(spread_grid, where_axis)
    grid_x, grid_y, grid_z = (8 * cells_x, 8 * cells_y, 8 * cells_z)
    fine_charge = spread_grid[9 : 9 + grid_x, 9 : 9 + grid_y, 9 : 9 + grid_z]
    halo_depth = 10
    widened = padded_2(fine_charge, (("gx", 0), ("gy", 1), ("ga", 2)), halo_depth)
    fine_potential = convolve(widened, fine_spread, fine_scale)
    coarse_charge = widened
    for where_axis, fine_length in enumerate((grid_x, grid_y, grid_z)):
        coarse_charge = along_axis(
            coarse_charge,
            grid_map(fine_length + 2 * halo_depth, fine_length // 2, -halo_depth, 0),
            where_axis,
        )
    grown_coarse = padded_2(coarse_charge, (("gx", 0), ("gy", 1), ("ga", 2)), 8)
    coarse_potential = convolve(grown_coarse, coarse_spread, coarse_scale)
    coarse_near = padded_2(coarse_potential, (("gx", 0), ("gy", 1), ("ga", 2)), 2)
    potential = coarse_near
    for where_axis, fine_length in enumerate((grid_x, grid_y, grid_z)):
        potential = along_axis(
            potential,
            jnp.transpose(grid_map(fine_length + 4, fine_length // 2 + 4, -2, -2)),
            where_axis,
        )
    inside_x = inside_grid(grid_x, lax.axis_index("gx") * grid_x, lax.axis_size("gx"))
    inside_y = inside_grid(grid_y, lax.axis_index("gy") * grid_y, lax.axis_size("gy"))
    inside_z = inside_grid(grid_z, lax.axis_index("ga") * grid_z, lax.axis_size("ga"))
    inside_mask = inside_x[:, None, None] * inside_y[None, :, None] * inside_z[None, None, :]
    potential = (potential + fine_potential) * inside_mask
    for where_axis in range(3):
        potential = cut_patches(potential, 2 * where_axis)
    near_grid = jnp.transpose(potential, (0, 2, 4, 1, 3, 5))
    long_force = grid_force(near_grid, weighted, offsets)
    return (short_force, long_force)


def solution(mesh):
    return jax.shard_map(
        per_device,
        mesh=mesh,
        in_specs=(
            P(None, "gx", "gy", "ga", None),
            P("gx", "gy", "ga", None),
            P("gx", "gy", "ga"),
            P("gx", "gy", "ga", None),
        ),
        out_specs=(P(None, "gx", "gy", "ga", None), P(None, "gx", "gy", "ga", None)),
        check_vma=False,
    )
```

profile of v0, /device:TPU:1, one launch (start us, length us, event | category | flops | bytes accessed | tf_op | source)
XLA Modules:
  0.0 534.6 jit_solution(4229664414464727326)
XLA Ops:
  21.1 5.5 %collective-permute-start.2 = (f32[4,4,1,16,128]{4,2,3,1,0:T(1,128)S(1)}, f32[4,4,1,16,128]{4,2,3,1,0:T(1,128)S(1)}, u32[]{:S(2)}, u32[]{:S(2)}) collective-permute-start(f32[4,4,1,16,128]{4,2,3,1,0:T(1,128)S(1)} %get-tuple-element.146), channel_id=1, source_target_pairs={{0,2},{2,4},{4,6},{6,8},{8,10},{10,12},{12,14},{1,3},{3,5},{5,7},{... | collective-permute-start | bytes 393224 | tf_op jit(solution)/shard_map/ppermute | solution.py:23
  28.6 5.5 %collective-permute-done.3 = f32[4,4,1,16,128]{4,2,3,1,0:T(1,128)S(1)} collective-permute-done((f32[4,4,1,16,128]{4,2,3,1,0:T(1,128)S(1)}, f32[4,4,1,16,128]{4,2,3,1,0:T(1,128)S(1)}, u32[]{:S(2)}, u32[]{:S(2)}) %collective-permute-start.3) | collective-permute-done | bytes 131104 | tf_op jit(solution)/shard_map/ppermute | solution.py:24
  50.6 30.1 %fusion.5 = f32[4,4,18,121,11]{3,4,2,1,0:T(8,128)S(1)} fusion(f32[4,4,18,128,121]{3,1,4,2,0:T(4,128)S(1)} %bitcast.113, f32[4,4,18,128]{3,2,1,0:T(8,128)S(1)} %copy.229, f32[11]{0:T(128)S(1)} %iota_convert_fusion), kind=kOutput, calls=%fused_computation.91 | convolution fusion | flops 592846848 | bytes 19522988 | tf_op jit(solution)/shard_map/...sp,...sc->...pc/dot_general | solution.py:53
  80.7 13.9 %copy.231 = f32[4,4,18,121,11]{2,1,4,3,0:T(4,128)} copy(f32[4,4,18,121,11]{3,4,2,1,0:T(8,128)S(1)} %fusion.5) | data formatting | bytes 3066624 | tf_op jit(solution)/shard_map/...sp,...sc->...pc/dot_general | solution.py:53
  94.6 7.7 %slice.358 = f32[4,8,4,11,18,11]{4,2,5,3,1,0:T(4,128)} slice(f32[4,11,4,11,18,11]{4,2,5,3,1,0:T(4,128)} %bitcast.114), slice={[0:4], [0:8], [0:4], [0:11], [0:18], [0:11]} | slice | bytes 2230272 | tf_op jit(solution)/shard_map/slice | solution.py:59
  104.6 9.5 %pad_add_fusion = f32[5,8,4,11,18,11]{4,2,5,3,1,0:T(4,128)} fusion(f32[4,3,4,11,18,11]{4,2,5,3,1,0:T(4,128)S(1)} %slice.359, f32[4,8,4,11,18,11]{4,2,5,3,1,0:T(4,128)} %slice.358), kind=kLoop, calls=%fused_computation.94 | loop fusion | flops 348480 | bytes 2927232 | tf_op jit(solution)/shard_map/add | solution.py:66
  128.6 6.2 %copy.262 = f32[40,40,18,8]{1,3,2,0:T(8,128)S(1)} copy(f32[40,40,18,8]{2,0,3,1:T(8,128)} %slice.362) | data formatting | bytes 1843200
  143.2 6.0 %collective-permute-start.6 = (f32[10,16,128]{2,0,1:T(8,128)S(1)}, f32[10,16,128]{2,0,1:T(8,128)S(1)}, u32[]{:S(2)}, u32[]{:S(2)}) collective-permute-start(f32[10,16,128]{2,0,1:T(8,128)S(1)} %copy.264), channel_id=1, source_target_pairs={{0,16},{16,32},{32,48},{48,64},{64,80},{80,96},{96,112},{1,17},{17... | collective-permute-start | bytes 245768 | tf_op jit(solution)/shard_map/ppermute | solution.py:23
  162.9 4.7 collective-permute-done.8
  181.6 6.5 %collective-permute-start.12 = (f32[8,8,64]{2,1,0:T(8,128)}, f32[8,8,64]{2,1,0:T(8,128)}, u32[]{:S(2)}, u32[]{:S(2)}) collective-permute-start(f32[8,8,64]{2,1,0:T(8,128)} %fusion.112), channel_id=1, source_target_pairs={{0,16},{16,32},{32,48},{48,64},{64,80},{80,96},{96,112},{1,17},{17... | collective-permute-start | bytes 49160 | tf_op jit(solution)/shard_map/ppermute | solution.py:23
  190.1 242.1 %while.10 = (s32[]{:T(128)}, f32[2,3,2,2,8,128]{5,4,3,2,1,0:T(8,128)}, s32[2]{0:T(128)S(1)}, f32[4,4,18,128]{3,2,1,0:T(8,128)S(1)}, f32[3,4,4,18,128]{4,2,3,1,0:...) while((s32[]{:T(128)}, f32[2,3,2,2,8,128]{5,4,3,2,1,0:T(8,128)}, s32[2]{0:T(128)S(1)}, ...), condition=%wide.region_3.4_spmd, body=%wide.region_0.3_spmd.sunk | while | flops 353894400 | bytes 236896768 | solution.py:210
  193.8 41.3 %fusion.304 = f32[2,2,8,128,3456]{4,3,2,1,0:T(8,128)} fusion(f32[3,2,2,8,3456]{4,3,2,1,0:T(8,128)S(1)} %constant_dynamic-update-slice_fusion.132, f32[3,2,2,8,128]{4,3,2,1,0:T(8,128)S(1)} %get-tuple-element.262), kind=kLoop, calls=%fused_computation.2.clone.1 | loop fusion | flops 113246208 | bytes 57999360 | tf_op jit(solution)/shard_map/while/body/eval_jaxpr/reduce_sum | solution.py:126
  235.7 36.7 %fusion.305 = f32[2,2,8,128,3456]{4,3,2,1,0:T(8,128)} fusion(f32[2,2,8,128,3456]{4,3,2,1,0:T(8,128)} %fusion.304, f32[2,2,8,3456]{3,2,1,0:T(8,128)S(1)} %constant_dynamic-update-slice_fusion.159), kind=kLoop, calls=%fused_computation.6.clone.1 | loop fusion | flops 113246208 | bytes 113688576 | tf_op jit(solution)/shard_map/while/body/eval_jaxpr/mul | solution.py:129
  272.4 38.0 %fusion.306 = f32[3,2,2,8,128]{4,3,2,1,0:T(8,128)S(1)} fusion(f32[2,2,8,128,3456]{4,3,2,1,0:T(8,128)} %fusion.305, f32[3,2,2,8,3456]{4,3,2,1,0:T(8,128)S(1)} %constant_dynamic-update-slice_fusion.132, f32[3,2,2,8,128]{4,3,2,1,0:T(8,128)S(1)} %get-tuple-element.262), kind=kLoop, calls=%fused_computation.3.clone.1 | loop fusion | flops 127389696 | bytes 58048512 | tf_op jit(solution)/shard_map/while/body/eval_jaxpr/reduce_sum | solution.py:131
  314.8 41.3 %fusion.304 = f32[2,2,8,128,3456]{4,3,2,1,0:T(8,128)} fusion(f32[3,2,2,8,3456]{4,3,2,1,0:T(8,128)S(1)} %constant_dynamic-update-slice_fusion.132, f32[3,2,2,8,128]{4,3,2,1,0:T(8,128)S(1)} %get-tuple-element.262), kind=kLoop, calls=%fused_computation.2.clone.1 | loop fusion | flops 113246208 | bytes 57999360 | tf_op jit(solution)/shard_map/while/body/eval_jaxpr/reduce_sum | solution.py:126
  356.7 36.7 %fusion.305 = f32[2,2,8,128,3456]{4,3,2,1,0:T(8,128)} fusion(f32[2,2,8,128,3456]{4,3,2,1,0:T(8,128)} %fusion.304, f32[2,2,8,3456]{3,2,1,0:T(8,128)S(1)} %constant_dynamic-update-slice_fusion.159), kind=kLoop, calls=%fused_computation.6.clone.1 | loop fusion | flops 113246208 | bytes 113688576 | tf_op jit(solution)/shard_map/while/body/eval_jaxpr/mul | solution.py:129
  393.5 38.0 %fusion.306 = f32[3,2,2,8,128]{4,3,2,1,0:T(8,128)S(1)} fusion(f32[2,2,8,128,3456]{4,3,2,1,0:T(8,128)} %fusion.305, f32[3,2,2,8,3456]{4,3,2,1,0:T(8,128)S(1)} %constant_dynamic-update-slice_fusion.132, f32[3,2,2,8,128]{4,3,2,1,0:T(8,128)S(1)} %get-tuple-element.262), kind=kLoop, calls=%fused_computation.3.clone.1 | loop fusion | flops 127389696 | bytes 58048512 | tf_op jit(solution)/shard_map/while/body/eval_jaxpr/reduce_sum | solution.py:131
  433.0 4.6 collective-permute-start.14
  457.2 5.7 %collective-permute-start.18 = (f32[2,8,64]{2,1,0:T(8,128)S(1)}, f32[2,8,64]{2,1,0:T(8,128)S(1)}, u32[]{:S(2)}, u32[]{:S(2)}) collective-permute-start(f32[2,8,64]{2,1,0:T(8,128)S(1)} %get-tuple-element.163), channel_id=1, source_target_pairs={{0,16},{16,32},{32,48},{48,64},{64,80},{80,96},{96,112},{1,17},{17... | collective-permute-start | bytes 12296 | tf_op jit(solution)/shard_map/ppermute | solution.py:23
  467.9 5.1 collective-permute-start.20
  497.0 6.3 %maximum_bitcast_fusion = f32[2,2,16,11,11,11]{5,2,1,4,3,0:T(8,128)} fusion(f32[2,11,2,11,16,3]{5,4,2,3,1,0:T(8,128)} %bitcast.123, f32[2,11,2,11,16,8]{5,4,2,3,1,0:T(8,128)} %reshape.347), kind=kLoop, calls=%fused_computation.106 | loop fusion | flops 85184 | bytes 681472 | tf_op jit(solution)/shard_map/transpose | solution.py:246
  503.3 7.2 %copy.250 = f32[2,2,16,11,11,11]{2,1,5,4,3,0:T(2,128)S(1)} copy(f32[2,2,16,11,11,11]{5,2,1,4,3,0:T(8,128)} %maximum_bitcast_fusion) | data formatting | bytes 681472 | tf_op jit(solution)/shard_map/transpose | solution.py:246
  514.0 9.6 %fusion.7 = f32[2,2,16,128]{3,2,1,0:T(8,128)S(1)} fusion(f32[2,2,16,128,121]{3,2,4,1,0:T(8,128)} %bitcast.122, f32[2,2,16,121,11]{3,4,2,1,0:T(8,128)} %copy.251, f32[2,2,16,128]{3,2,1,0:T(8,128)S(1)} %copy-done.19, f32[11]{0:T(128)S(1)} %copy-done.29), kind=kOutput, calls=%fused_computation.98 | convolution fusion | flops 133718016 | bytes 4371244 | tf_op jit(solution)/shard_map/...pc,...sc->...sp/dot_general | solution.py:148
  523.6 10.1 %fusion.9 = (f32[2,2,16,128]{3,2,1,0:T(8,128)S(1)}, f32[2,2,16,128]{3,2,1,0:T(8,128)S(1)}) fusion(f32[2,2,16,128,121]{3,2,4,1,0:T(8,128)} %bitcast.121, f32[2,2,16,128,121]{3,2,4,1,0:T(8,128)S(1)} %bitcast.120, f32[2,2,16,121,11]{3,4,2,1,0:T(8,128)S(1)} %copy-done.4, f32[2,2,16,128]{3,2,1,0:T(8,128)S(1)} %copy-done.19, f32[11]{0:T(128)S(1)} %copy-done.29), kind=kOutput, calls=%fused_computation.102 | convolution fusion | flops 135692288 | bytes 8368940 | tf_op jit(solution)/shard_map/...pc,...sc->...sp/dot_general | solution.py:147
  (341 shorter events, 151.4 us)
Async XLA Ops:
  6.1 14.7 %collective-permute-start = (f32[4,1,2,16,128]{4,2,3,1,0:T(2,128)S(1)}, f32[4,1,2,16,128]{4,2,3,1,0:T(2,128)S(1)}, u32[]{:S(2)}, u32[]{:S(2)}) collective-permute-start(f32[4,1,2,16,128]{4,2,3,1,0:T(2,128)S(1)} %get-tuple-element.148), channel_id=1, source_target_pairs={{0,16},{16,32},{32,48},{48,64},{64,80},{80,96},{96,112},{1,17},{17... | collective-permute-start | bytes 196616 | tf_op jit(solution)/shard_map/ppermute | solution.py:23
  10.7 10.1 %collective-permute-start.1 = (f32[4,1,2,16,128]{4,2,3,1,0:T(2,128)S(1)}, f32[4,1,2,16,128]{4,2,3,1,0:T(2,128)S(1)}, u32[]{:S(2)}, u32[]{:S(2)}) collective-permute-start(f32[4,1,2,16,128]{4,2,3,1,0:T(2,128)S(1)} %get-tuple-element.149), channel_id=1, source_target_pairs={{16,0},{32,16},{48,32},{64,48},{80,64},{96,80},{112,96},{17,1},{33... | collective-permute-start | bytes 196616 | tf_op jit(solution)/shard_map/ppermute | solution.py:24
  21.1 7.4 %collective-permute-start.2 = (f32[4,4,1,16,128]{4,2,3,1,0:T(1,128)S(1)}, f32[4,4,1,16,128]{4,2,3,1,0:T(1,128)S(1)}, u32[]{:S(2)}, u32[]{:S(2)}) collective-permute-start(f32[4,4,1,16,128]{4,2,3,1,0:T(1,128)S(1)} %get-tuple-element.146), channel_id=1, source_target_pairs={{0,2},{2,4},{4,6},{6,8},{8,10},{10,12},{12,14},{1,3},{3,5},{5,7},{... | collective-permute-start | bytes 393224 | tf_op jit(solution)/shard_map/ppermute | solution.py:23
  26.6 7.4 %collective-permute-start.3 = (f32[4,4,1,16,128]{4,2,3,1,0:T(1,128)S(1)}, f32[4,4,1,16,128]{4,2,3,1,0:T(1,128)S(1)}, u32[]{:S(2)}, u32[]{:S(2)}) collective-permute-start(f32[4,4,1,16,128]{4,2,3,1,0:T(1,128)S(1)} %get-tuple-element.147), channel_id=1, source_target_pairs={{2,0},{4,2},{6,4},{8,6},{10,8},{12,10},{14,12},{3,1},{5,3},{7,5},{... | collective-permute-start | bytes 393224 | tf_op jit(solution)/shard_map/ppermute | solution.py:24
  34.1 5.1 collective-permute-start.4
  36.7 5.1 collective-permute-start.5
  143.2 10.2 %collective-permute-start.6 = (f32[10,16,128]{2,0,1:T(8,128)S(1)}, f32[10,16,128]{2,0,1:T(8,128)S(1)}, u32[]{:S(2)}, u32[]{:S(2)}) collective-permute-start(f32[10,16,128]{2,0,1:T(8,128)S(1)} %copy.264), channel_id=1, source_target_pairs={{0,16},{16,32},{32,48},{48,64},{64,80},{80,96},{96,112},{1,17},{17... | collective-permute-start | bytes 245768 | tf_op jit(solution)/shard_map/ppermute | solution.py:23
  149.5 6.3 %collective-permute-start.7 = (f32[10,16,128]{2,0,1:T(8,128)S(1)}, f32[10,16,128]{2,0,1:T(8,128)S(1)}, u32[]{:S(2)}, u32[]{:S(2)}) collective-permute-start(f32[10,16,128]{2,0,1:T(8,128)S(1)} %copy.266), channel_id=1, source_target_pairs={{16,0},{32,16},{48,32},{64,48},{80,64},{96,80},{112,96},{17,1},{33... | collective-permute-start | bytes 245768 | tf_op jit(solution)/shard_map/ppermute | solution.py:24
  155.9 11.7 %collective-permute-start.8 = (f32[36,10,128]{2,0,1:T(8,128)S(1)}, f32[36,10,128]{2,0,1:T(8,128)S(1)}, u32[]{:S(2)}, u32[]{:S(2)}) collective-permute-start(f32[36,10,128]{2,0,1:T(8,128)S(1)} %get-tuple-element.142), channel_id=1, source_target_pairs={{0,2},{2,4},{4,6},{6,8},{8,10},{10,12},{12,14},{1,3},{3,5},{5,7},{... | collective-permute-start | bytes 552968 | tf_op jit(solution)/shard_map/ppermute | solution.py:23
  160.5 8.0 %collective-permute-start.9 = (f32[36,10,128]{2,0,1:T(8,128)S(1)}, f32[36,10,128]{2,0,1:T(8,128)S(1)}, u32[]{:S(2)}, u32[]{:S(2)}) collective-permute-start(f32[36,10,128]{2,0,1:T(8,128)S(1)} %get-tuple-element.143), channel_id=1, source_target_pairs={{2,0},{4,2},{6,4},{8,6},{10,8},{12,10},{14,12},{3,1},{5,3},{7,5},{... | collective-permute-start | bytes 552968 | tf_op jit(solution)/shard_map/ppermute | solution.py:24
  169.3 4.7 collective-permute-start.10
  170.9 7.5 %collective-permute-start.11 = (f32[36,36,10]{1,0,2:T(8,128)S(1)}, f32[36,36,10]{1,0,2:T(8,128)S(1)}, u32[]{:S(2)}, u32[]{:S(2)}) collective-permute-start(f32[36,36,10]{1,0,2:T(8,128)S(1)} %copy.239), channel_id=1, source_target_pairs={{1,0},{3,2},{5,4},{7,6},{9,8},{11,10},{13,12},{15,14},{17,16},{19,... | collective-permute-start | bytes 155528 | tf_op jit(solution)/shard_map/ppermute | solution.py:24
  181.6 250.6 %collective-permute-start.12 = (f32[8,8,64]{2,1,0:T(8,128)}, f32[8,8,64]{2,1,0:T(8,128)}, u32[]{:S(2)}, u32[]{:S(2)}) collective-permute-start(f32[8,8,64]{2,1,0:T(8,128)} %fusion.112), channel_id=1, source_target_pairs={{0,16},{16,32},{32,48},{48,64},{64,80},{80,96},{96,112},{1,17},{17... | collective-permute-start | bytes 49160 | tf_op jit(solution)/shard_map/ppermute | solution.py:23
  188.2 244.1 %collective-permute-start.13 = (f32[8,8,64]{2,1,0:T(8,128)}, f32[8,8,64]{2,1,0:T(8,128)}, u32[]{:S(2)}, u32[]{:S(2)}) collective-permute-start(f32[8,8,64]{2,1,0:T(8,128)} %fusion.112), channel_id=1, source_target_pairs={{16,0},{32,16},{48,32},{64,48},{80,64},{96,80},{112,96},{17,1},{33... | collective-permute-start | bytes 49160 | tf_op jit(solution)/shard_map/ppermute | solution.py:24
  433.0 11.1 %collective-permute-start.14 = (f32[24,8,64]{2,1,0:T(8,128)S(1)}, f32[24,8,64]{2,1,0:T(8,128)S(1)}, u32[]{:S(2)}, u32[]{:S(2)}) collective-permute-start(f32[24,8,64]{2,1,0:T(8,128)S(1)} %pad_maximum_fusion.10), channel_id=1, source_target_pairs={{0,2},{2,4},{4,6},{6,8},{8,10},{10,12},{12,14},{1,3},{3,5},{5,7},{... | collective-permute-start | bytes 147464 | tf_op jit(solution)/shard_map/ppermute | solution.py:23
  437.7 6.9 %collective-permute-start.15 = (f32[24,8,64]{2,1,0:T(8,128)S(1)}, f32[24,8,64]{2,1,0:T(8,128)S(1)}, u32[]{:S(2)}, u32[]{:S(2)}) collective-permute-start(f32[24,8,64]{2,1,0:T(8,128)S(1)} %pad_maximum_fusion.10), channel_id=1, source_target_pairs={{2,0},{4,2},{6,4},{8,6},{10,8},{12,10},{14,12},{3,1},{5,3},{7,5},{... | collective-permute-start | bytes 147464 | tf_op jit(solution)/shard_map/ppermute | solution.py:24
  445.5 5.8 %collective-permute-start.16 = (f32[24,24,8]{2,1,0:T(8,128)S(1)}, f32[24,24,8]{2,1,0:T(8,128)S(1)}, u32[]{:S(2)}, u32[]{:S(2)}) collective-permute-start(f32[24,24,8]{2,1,0:T(8,128)S(1)} %get-tuple-element.144), channel_id=1, source_target_pairs={{0,1},{2,3},{4,5},{6,7},{8,9},{10,11},{12,13},{14,15},{16,17},{18,... | collective-permute-start | bytes 55304 | tf_op jit(solution)/shard_map/ppermute | solution.py:23
  446.8 8.6 %collective-permute-start.17 = (f32[24,24,8]{2,1,0:T(8,128)S(1)}, f32[24,24,8]{2,1,0:T(8,128)S(1)}, u32[]{:S(2)}, u32[]{:S(2)}) collective-permute-start(f32[24,24,8]{2,1,0:T(8,128)S(1)} %get-tuple-element.145), channel_id=1, source_target_pairs={{1,0},{3,2},{5,4},{7,6},{9,8},{11,10},{13,12},{15,14},{17,16},{19,... | collective-permute-start | bytes 55304 | tf_op jit(solution)/shard_map/ppermute | solution.py:24
  457.2 9.2 %collective-permute-start.18 = (f32[2,8,64]{2,1,0:T(8,128)S(1)}, f32[2,8,64]{2,1,0:T(8,128)S(1)}, u32[]{:S(2)}, u32[]{:S(2)}) collective-permute-start(f32[2,8,64]{2,1,0:T(8,128)S(1)} %get-tuple-element.163), channel_id=1, source_target_pairs={{0,16},{16,32},{32,48},{48,64},{64,80},{80,96},{96,112},{1,17},{17... | collective-permute-start | bytes 12296 | tf_op jit(solution)/shard_map/ppermute | solution.py:23
  462.9 5.0 collective-permute-start.19
  467.9 7.4 %collective-permute-start.20 = (f32[12,2,64]{2,1,0:T(2,128)S(1)}, f32[12,2,64]{2,1,0:T(2,128)S(1)}, u32[]{:S(2)}, u32[]{:S(2)}) collective-permute-start(f32[12,2,64]{2,1,0:T(2,128)S(1)} %get-tuple-element.157), channel_id=1, source_target_pairs={{0,2},{2,4},{4,6},{6,8},{8,10},{10,12},{12,14},{1,3},{3,5},{5,7},{... | collective-permute-start | bytes 18440 | tf_op jit(solution)/shard_map/ppermute | solution.py:23
  473.0 5.9 %collective-permute-start.21 = (f32[12,2,64]{2,1,0:T(2,128)S(1)}, f32[12,2,64]{2,1,0:T(2,128)S(1)}, u32[]{:S(2)}, u32[]{:S(2)}) collective-permute-start(f32[12,2,64]{2,1,0:T(2,128)S(1)} %get-tuple-element.158), channel_id=1, source_target_pairs={{2,0},{4,2},{6,4},{8,6},{10,8},{12,10},{14,12},{3,1},{5,3},{7,5},{... | collective-permute-start | bytes 18440 | tf_op jit(solution)/shard_map/ppermute | solution.py:24
  479.1 3.6 collective-permute-start.22
  480.4 6.7 %collective-permute-start.23 = (f32[12,12,2]{2,1,0:T(8,128)S(1)}, f32[12,12,2]{2,1,0:T(8,128)S(1)}, u32[]{:S(2)}, u32[]{:S(2)}) collective-permute-start(f32[12,12,2]{2,1,0:T(8,128)S(1)} %get-tuple-element.154), channel_id=1, source_target_pairs={{1,0},{3,2},{5,4},{7,6},{9,8},{11,10},{13,12},{15,14},{17,16},{19,... | collective-permute-start | bytes 3464 | tf_op jit(solution)/shard_map/ppermute | solution.py:24
  (40 other events, 844.7 us)
where the time goes:
time: 542 us; the launch traced here: 535 us
  other arithmetic  273 us (50%)
  local copies, waits for them, and re-layouts  83.5 us (15%)
  starting transfers between devices  67.8 us (13%)
  matrix products  64.2 us (12%)
  waiting for transfers between devices  38.7 us (7%)
    reduce_sum x2, other arithmetic, pair_sum(): distance_sq = jnp.sum(separation * separation, axis=0)  82.6 us
    reduce_sum x2, other arithmetic, pair_sum(): return own_charge * jnp.sum(separation * strength, axis=-1)  76.1 us
    mul x2, other arithmetic, pair_sum(): reach_left * reach_left * reach_left / (distance_sq + soften_sq)  73.4 us
    ppermute x12, starting transfers between devices, padded_2(): before = lax.ppermute(last, axis, up)  49.2 us
    dot_general x1, matrix products, charge_patches(): jnp.einsum('...sp,...sc->...pc', flattened, weight_z, precision=highest)  30.1 us
    ppermute x12, waiting for transfers between devices, padded_2(): after = lax.ppermute(initial, axis, down)  29.5 us
    ppermute x12, starting transfers between devices, padded_2(): after = lax.ppermute(initial, axis, down)  18.6 us
    unnamed x80, local copies, waits for them, and re-layouts  15.6 us
  transfers between devices with their start and end apart: 24, of which 15 were waited for; matrix products, arithmetic and copies ran while one was open for 48% of the time, Pallas kernels for 0%

commit v1 on v0

v1 whole, which is shorter than its diff:
```python
import jax
import jax.numpy as jnp
import numpy as np
from jax import lax
from jax.experimental import pallas as pl
from jax.experimental.pallas import tpu as pltpu
from jax.sharding import PartitionSpec as P

f32, bf16, i32 = jnp.float32, jnp.bfloat16, jnp.int32
LAST = (((1,), (1,)), ((), ()))
CAP = 65.0 / 64.0
ROWS, TILES, SLOTS = 64, 4, 4
VMEM = pl.BlockSpec(memory_space=pltpu.VMEM)
SMEM = pl.BlockSpec(memory_space=pltpu.SMEM)
ANY = pl.BlockSpec(memory_space=pl.ANY)


def fine_kernel(gap):
    return np.where(np.abs(gap) <= 8, np.exp(-gap * gap / 12.5), 0.0)


def coarse_kernel(gap):
    return np.where(np.abs(gap) <= 8, np.exp(-gap * gap / 72.0), 0.0)


def hat(gap):
    return np.where(gap == 0, 1.0, np.where(np.abs(gap) == 1, 0.5, 0.0))


def halves(matrix):
    high = matrix.astype(np.float32).astype(jnp.bfloat16)
    low = (matrix - high.astype(np.float64)).astype(np.float32).astype(jnp.bfloat16)
    return high, low


def z_operator(part):
    source = np.full(256, 10**6, np.int64)
    source[:131] = 128 * part - 1 + np.arange(131)
    source[160:181] = np.arange(21) + (127 if part == 0 else 109)
    inside = (source >= 0) & (source < 256)
    result = np.zeros((256, 256))
    target = 128 * part - 1 + np.arange(131)
    fine = fine_kernel((target[None, :] - source[:, None]).astype(np.float64))
    result[:, :131] = fine * ((target >= 0) & (target < 256))[None, :]
    middle = np.arange(128)
    down = hat((source[:, None] - 2 * middle[None, :]).astype(np.float64))
    point = 64 * part - 1 + np.arange(67)
    spread = coarse_kernel((middle[:, None] - point[None, :]).astype(np.float64))
    spread = spread * ((point >= 0) & (point < 128))[None, :]
    result[:, 136:203] = down @ spread
    return result * inside[:, None]


def y_operators():
    own = np.where(np.arange(24) < 19, np.arange(24), 10**6)
    below = np.where(np.arange(16) < 11, np.arange(16) - 8, 10**6)
    above = np.where(np.arange(16) < 11, np.arange(16) + 16, 10**6)
    source = np.concatenate([own, below, above]).astype(np.float64)
    fine = fine_kernel(np.arange(24)[:, None] - source[None, :])
    fine[19:] = 0
    own = np.where(np.arange(16) < 11, np.arange(16), 10**6)
    below = np.where(np.arange(16) < 11, np.arange(16) - 8, 10**6)
    above = np.where(np.arange(16) < 11, np.arange(16) + 8, 10**6)
    far_below = np.where(np.arange(8) < 3, np.arange(8) - 8, 10**6)
    far_above = np.where(np.arange(8) < 3, np.arange(8) + 16, 10**6)
    source = np.concatenate([own, below, above, far_below, far_above]).astype(np.float64)
    coarse = coarse_kernel(np.arange(16)[:, None] - source[None, :])
    coarse[11:] = 0
    down = hat(np.arange(24)[None, :] - (2.0 * np.arange(16)[:, None] - 1))
    down[11:] = 0
    up = hat(np.arange(24)[:, None] - (2.0 * np.arange(16)[None, :] - 1))
    up[19:] = 0
    up[:, 11:] = 0
    stack = lambda m: np.concatenate([halves(m)[0], halves(m)[1], halves(m)[0]], 1)
    thrice = lambda m: np.concatenate([halves(m)[0]] * 3, 1)
    return stack(fine), stack(coarse), thrice(down), thrice(up)


def z_prolong():
    result = np.zeros((128, 256))
    point = 2.0 * np.arange(67) - 1
    result[8:75, :131] = hat(np.arange(131)[None, :] - point[:, None])
    return halves(result)[0]


def split2(value):
    high = value.astype(bf16)
    return high, (value - high.astype(f32)).astype(bf16)


def split3(value):
    high = value.astype(bf16).astype(f32)
    rest = value - high
    middle = rest.astype(bf16).astype(f32)
    return high, middle, rest - middle


def dot(left, right):
    return jnp.dot(left, right, preferred_element_type=f32)


def spline(shifted):
    magnitude = jnp.abs(shifted)
    margin = jnp.maximum(1.5 - magnitude, 0.0)
    return jnp.where(magnitude < 0.5, 0.75 - shifted * shifted, 0.5 * margin * margin)


def spline_slope(shifted):
    magnitude = jnp.abs(shifted)
    margin = jnp.maximum(1.5 - magnitude, 0.0)
    return jnp.where(magnitude < 0.5, -2.0 * shifted, jnp.where(shifted > 0.0, -margin, margin))


def weights_at(offset, rows, first):
    points = lax.broadcasted_iota(i32, (rows, 128), 0).astype(f32)
    return 8.0 * offset + (1.0 + first) - points


def inside_mask(shape, dim, start, count):
    point = lax.broadcasted_iota(i32, shape, dim) + start
    return ((point >= 0) & (point < count)).astype(f32)


def spread_kernel(off_ref, charge_ref, counts_ref, block_ref, near_ref, rho_ref, msg_ref):
    dx, dy, dz = lax.axis_index("gx"), lax.axis_index("gy"), lax.axis_index("ga")
    lane = lax.broadcasted_iota(i32, (1, 128), 1)
    row8 = lax.broadcasted_iota(i32, (8, 128), 0)
    rho_ref[...] = jnp.zeros((19, 24, 256), f32)
    zero8 = jnp.zeros((8, 128), f32)
    for i in range(2):
        for j in range(2):
            near_ref[i, j, 0] = zero8
            near_ref[i, j, 17] = zero8

    def column(ij, _):
        i, j = ij >> 1, ij & 1
        shift_x = 8.0 * (i + 1).astype(f32)
        shift_y = 8.0 * (j + 1).astype(f32)
        total = jnp.zeros((176, 128), f32)
        tail = None
        for m in range(8):
            highs, lows, z_highs, z_lows = [], [], [], []
            for half in range(2):
                k = 2 * m + half
                ox = off_ref[0, i, j, k : k + 1]
                oy = off_ref[1, i, j, k : k + 1]
                oz = off_ref[2, i, j, k : k + 1]
                count = counts_ref[ij * 16 + k]
                weighted = jnp.where(lane < count, charge_ref[i, j, k : k + 1], 0.0)
                near_ref[i, j, k + 1] = jnp.concatenate(
                    [8.0 * ox + shift_x, 8.0 * oy + shift_y, 8.0 * oz + 8.0 * (k + 1), weighted, zero8[:4]], 0
                )
                wx = spline(weights_at(ox, 16, 0)) * weighted
                wy = spline(weights_at(oy, 16, 0))
                wz = spline(weights_at(oz, 32, 8 * half))
                plane = jnp.concatenate([wx[a : a + 1] * wy for a in range(11)], 0)
                high, low = split2(plane)
                highs.append(high)
                lows.append(low)
                z_high, z_low = split2(wz)
                z_highs.append(z_high)
                z_lows.append(z_low)
            left = jnp.concatenate(highs + lows + highs, 1)
            right = jnp.concatenate(z_highs + z_highs + z_lows, 1)
            if m < 7:
                pieces = [right]
                if m > 0:
                    pieces = [jnp.zeros((16 * m, 768), bf16)] + pieces
                if m < 6:
                    pieces = pieces + [jnp.zeros((96 - 16 * m, 768), bf16)]
                total = total + lax.dot_general(left, jnp.concatenate(pieces, 0), LAST, preferred_element_type=f32)
            else:
                wide = jnp.concatenate([jnp.zeros((112, 768), bf16), right, jnp.zeros((112, 768), bf16)], 0)
                both = lax.dot_general(left, wide, LAST, preferred_element_type=f32)
                total = total + both[:, :128]
                tail = both[:, 128:]
        first = pl.multiple_of(8 * j, 8)
        for a in range(11):
            rho_ref[8 * i + a, pl.ds(first, 16), 0:128] += total[16 * a : 16 * a + 16]
            rho_ref[8 * i + a, pl.ds(first, 16), 128:256] += tail[16 * a : 16 * a + 16]
        return 0

    lax.fori_loop(0, 4, column, 0)
    mask_y = inside_mask((24, 256), 0, 16 * dy - 1, 128)
    mask_z = inside_mask((24, 256), 1, 128 * dz - 1, 256)
    mask = mask_y * mask_z
    wide_lane = lax.broadcasted_iota(i32, (24, 128), 1)
    msg_ref[0:8] = block_ref[...]
    for i in range(2):
        picked = [jnp.where(dz == 0, near_ref[i, j, 16], near_ref[i, j, 1]) for j in range(2)]
        msg_ref[8 + 8 * i : 16 + 8 * i] = jnp.where(row8 < 4, picked[0], pltpu.roll(picked[1], 4, 0))
    faces = []
    for a in range(19):
        point = 16 * dx - 1 + a
        keep = ((point >= 0) & (point < 128)).astype(f32)
        plane = rho_ref[a] * (mask * keep)
        rho_ref[a] = plane
        low, high = plane[:, :128], plane[:, 128:]
        top = jnp.where(wide_lane < 18, pltpu.roll(low, 18, 1), pltpu.roll(high, 18, 1))
        face = jnp.where(dz == 0, top, low)
        faces.append(jnp.where(wide_lane < 21, face, 0.0))
    faces.append(jnp.zeros((24, 128), f32))
    for p in range(5):
        packed = faces[p]
        for g in range(1, 4):
            packed = packed + pltpu.roll(faces[5 * g + p], 32 * g, 1)
        msg_ref[24 + 24 * p : 48 + 24 * p] = packed


def along_z_kernel(near_ref, rho_ref, own_msg_ref, got_ref, op_ref, down_ref,
                   near1_ref, full_ref, restr_ref, up_ref, dn_ref, up2_ref, dn2_ref):
    dy, dz = lax.axis_index("gy"), lax.axis_index("ga")
    row8 = lax.broadcasted_iota(i32, (8, 128), 0)
    shift = jnp.where(row8 == 2, jnp.where(dz == 0, 128.0, -128.0), 0.0)
    for i in range(2):
        got = got_ref[8 + 8 * i : 16 + 8 * i]
        parts = [jnp.where(row8 < 4, got, 0.0), jnp.where(row8 < 4, pltpu.roll(got, 4, 0), 0.0)]
        for j in range(2):
            near1_ref[i, j, 1:17] = near_ref[i, j, 1:17]
            moved = parts[j] + shift
            near1_ref[i, j, 0] = jnp.where(dz == 1, moved, 0.0)
            near1_ref[i, j, 17] = jnp.where(dz == 0, moved, 0.0)
    lane = lax.broadcasted_iota(i32, (24, 128), 1)
    high_op, low_op = op_ref[dz, 0], op_ref[dz, 1]
    down = down_ref[...]
    lane16 = lax.broadcasted_iota(i32, (16, 128), 1)
    keep = inside_mask((16, 128), 0, 8 * dy - 1, 64)
    for g in range(4):
        planes = range(5 * g, min(5 * g + 5, 19))
        stacked = []
        for p, a in enumerate(planes):
            face = pltpu.roll(got_ref[24 + 24 * p : 48 + 24 * p], (32 - 32 * g) % 128, 1)
            second = jnp.where((lane >= 32) & (lane < 64), face, rho_ref[a, :, 128:256])
            stacked.append(jnp.concatenate([rho_ref[a, :, 0:128], second], 1))
        high, low = split2(jnp.concatenate(stacked, 0))
        result = dot(high, high_op) + dot(low, high_op) + dot(high, low_op)
        for p, a in enumerate(planes):
            plane = result[24 * p : 24 * p + 24]
            full_ref[a] = plane
            h, m, l = split3(plane[:, 128:256])
            restricted = dot(down, jnp.concatenate([h, m, l], 0).astype(bf16)) * keep
            restr_ref[a] = restricted
            for out, first in ((up_ref, 8), (dn_ref, 0)):
                out[152 + 16 * a : 168 + 16 * a] = plane[first : first + 16, 0:128]
                out[456 + 16 * a : 472 + 16 * a] = jnp.where(
                    lane16 < 8, plane[first : first + 16, 128:256], restricted
                )
            up2_ref[8 * a : 8 * a + 8] = restricted[8:16]
            dn2_ref[8 * a : 8 * a + 8] = restricted[0:8]
    counts = jnp.where(row8 == 0, own_msg_ref[0:8], jnp.where(row8 == 1, pltpu.roll(got_ref[0:8], 1, 0), 0.0))
    for out, j in ((up_ref, 1), (dn_ref, 0)):
        out[0:8] = counts
        for level in range(18):
            out[8 + 8 * level : 16 + 8 * level] = jnp.where(
                row8 < 4, near1_ref[0, j, level], pltpu.roll(near1_ref[1, j, level], 4, 0)
            )


def along_y_kernel(near1_ref, full_ref, restr_ref, up_own_ref, below_ref, above_ref, below2_ref, above2_ref,
                   fine_ref, coarse_ref, after_ref, near2_ref, fine2_ref, coarse2_ref,
                   up_ref, dn_ref, up2_ref, dn2_ref):
    dx, dy = lax.axis_index("gx"), lax.axis_index("gy")
    row8 = lax.broadcasted_iota(i32, (8, 128), 0)
    keep = inside_mask((16, 128), 0, 8 * dy - 1, 64)
    lane16 = lax.broadcasted_iota(i32, (16, 128), 1)
    lane24 = lax.broadcasted_iota(i32, (24, 128), 1)
    fine_op, coarse_op = fine_ref[...], coarse_ref[...]

    def plane(a, _):
        at = pl.multiple_of(16 * a, 16)
        at8 = pl.multiple_of(8 * a, 8)
        below_low = below_ref[pl.ds(152 + at, 16)]
        below_high = below_ref[pl.ds(456 + at, 16)]
        above_low = above_ref[pl.ds(152 + at, 16)]
        above_high = above_ref[pl.ds(456 + at, 16)]
        stack = jnp.concatenate(
            [
                full_ref[a],
                jnp.concatenate([below_low, below_high], 1),
                jnp.concatenate([above_low, above_high], 1),
            ],
            0,
        )
        high, low = split3(stack)[:2]
        fine2_ref[a] = dot(fine_op, jnp.concatenate([high, high, low], 0).astype(bf16))
        stack = jnp.concatenate(
            [restr_ref[a], below_high, above_high, below2_ref[pl.ds(at8, 8)], above2_ref[pl.ds(at8, 8)]], 0
        )
        high, low = split3(stack)[:2]
        coarse2_ref[a] = dot(coarse_op, jnp.concatenate([high, high, low], 0).astype(bf16)) * keep
        return 0

    lax.fori_loop(0, 19, plane, 0)
    restricted = []
    for e in range(11):
        value = None
        for a, weight in ((2 * e - 2, 0.5), (2 * e - 1, 1.0), (2 * e, 0.5)):
            if 0 <= a < 19:
                term = coarse2_ref[a] * weight
                value = term if value is None else value + term
        point = 8 * dx - 1 + e
        restricted.append(value * ((point >= 0) & (point < 64)).astype(f32))
    blank = jnp.zeros((8, 128), f32)
    for out, first in ((up_ref, 8), (dn_ref, 0)):
        for n in range(11):
            plane_value = fine2_ref[first + n]
            out[296 + 24 * n : 320 + 24 * n] = plane_value[:, 0:128]
            out[560 + 24 * n : 584 + 24 * n] = jnp.where(
                lane24 < 8, plane_value[:, 128:256], jnp.concatenate([restricted[n], blank], 0)
            )
    for n in range(3):
        up2_ref[16 * n : 16 * n + 16] = restricted[8 + n]
        dn2_ref[16 * n : 16 * n + 16] = restricted[n]
    shift_down = jnp.where(row8 == 1, -16.0, 0.0)
    shift_up = jnp.where(row8 == 1, 16.0, 0.0)
    for level in range(18):
        for y, source, shift in ((0, below_ref, shift_down), (3, above_ref, shift_up)):
            got = source[8 + 8 * level : 16 + 8 * level]
            near2_ref[0, y, level] = jnp.where(row8 < 4, got, 0.0) + shift
            near2_ref[1, y, level] = jnp.where(row8 < 4, pltpu.roll(got, 4, 0), 0.0) + shift
        for x in range(2):
            for y in range(2):
                near2_ref[x, y + 1, level] = near1_ref[x, y, level]
    counts = jnp.where(row8 < 2, up_own_ref[0:8], 0.0)
    counts = jnp.where((row8 >= 2) & (row8 < 4), pltpu.roll(below_ref[0:8], 2, 0), counts)
    counts = jnp.where((row8 >= 4) & (row8 < 6), pltpu.roll(above_ref[0:8], 4, 0), counts)
    for out, x in ((up_ref, 1), (dn_ref, 0)):
        out[0:8] = counts
        for level in range(18):
            for pair in range(2):
                at = 8 + 8 * (2 * level + pair)
                out[at : at + 8] = jnp.where(
                    row8 < 4, near2_ref[x, 2 * pair, level], pltpu.roll(near2_ref[x, 2 * pair + 1, level], 4, 0)
                )


def along_x_kernel(fine2_ref, up_own_ref, dn_own_ref, below_ref, above_ref, below2_ref, above2_ref,
                   up_y_ref, up_z_ref, after_ref, phi_ref, source, third, coarse):
    dx, dy, dz = lax.axis_index("gx"), lax.axis_index("gy"), lax.axis_index("ga")
    for p in range(35):
        rel = p - 8
        low = high = None
        pieces = []
        if 0 <= rel < 19:
            pieces.append((fine2_ref[rel, :, 0:128], fine2_ref[rel, :, 128:256]))
        if rel <= 2:
            n = rel + 8
            pieces.append((below_ref[296 + 24 * n : 320 + 24 * n], below_ref[560 + 24 * n : 584 + 24 * n]))
        if rel >= 16:
            n = rel - 16
            pieces.append((above_ref[296 + 24 * n : 320 + 24 * n], above_ref[560 + 24 * n : 584 + 24 * n]))
        for low_piece, high_piece in pieces:
            low = low_piece if low is None else low + low_piece
            high = high_piece if high is None else high + high_piece
        source[p, :, 0:128] = low
        source[p, :, 128:256] = high
    fine_weights = [float(w) for w in fine_kernel(np.arange(9.0))]
    coarse_weights = [float(w) for w in coarse_kernel(np.arange(9.0))]

    def fine_plane(a, _):
        value = source[a + 8] * (4.0 * fine_weights[0])
        for d in range(1, 9):
            value = value + (source[a + 8 - d] + source[a + 8 + d]) * (4.0 * fine_weights[d])
        third[a] = value
        return 0

    lax.fori_loop(0, 19, fine_plane, 0)

    def own_coarse(e):
        ref, n = (up_own_ref, e)
        return ref[560 + 24 * n : 576 + 24 * n]

    for p in range(27):
        rel = p - 8
        value = None
        pieces = []
        if 0 <= rel < 11:
            pieces.append(own_coarse(rel))
        if rel <= 2:
            n = rel + 8
            pieces.append(below_ref[560 + 24 * n : 576 + 24 * n])
        if rel >= 8:
            n = rel - 8
            pieces.append(above_ref[560 + 24 * n : 576 + 24 * n])
        if rel <= -6:
            n = rel + 8
            pieces.append(below2_ref[16 * n : 16 * n + 16])
        if rel >= 16:
            n = rel - 16
            pieces.append(above2_ref[16 * n : 16 * n + 16])
        for piece in pieces:
            value = piece if value is None else value + piece
        coarse[p] = value
    lifted = []
    up_y, up_z = up_y_ref[...], up_z_ref[...]
    for e in range(11):
        value = coarse[e + 8] * (2.0 * coarse_weights[0])
        for d in range(1, 9):
            value = value + (coarse[e + 8 - d] + coarse[e + 8 + d]) * (2.0 * coarse_weights[d])
        point = 8 * dx - 1 + e
        value = value * ((point >= 0) & (point < 64)).astype(f32)
        h, m, l = split3(value)
        tall = dot(up_y, jnp.concatenate([h, m, l], 0).astype(bf16))
        h, m, l = split3(tall)
        stacked = jnp.concatenate([h, m, l], 0).astype(bf16)
        wide = dot(stacked, up_z)
        lifted.append(wide[0:24] + wide[24:48] + wide[48:72])
    mask = inside_mask((24, 256), 0, 16 * dy - 1, 128) * inside_mask((24, 256), 1, 128 * dz - 1, 256)
    lane = lax.broadcasted_iota(i32, (24, 256), 1)
    mask = jnp.where(lane < 131, mask, 0.0)
    for a in range(19):
        if a % 2:
            value = lifted[(a + 1) // 2]
        else:
            value = 0.5 * (lifted[a // 2] + lifted[a // 2 + 1])
        point = 16 * dx - 1 + a
        keep = mask * ((point >= 0) & (point < 128)).astype(f32)
        phi_ref[a] = jnp.where(keep > 0.0, third[a] + value, 0.0)


def gather_kernel(off_ref, charge_ref, counts_ref, phi_ref, out_ref):
    lane = lax.broadcasted_iota(i32, (1, 128), 1)
    lane176 = lax.broadcasted_iota(i32, (176, 128), 1)

    def column(ij, _):
        i, j = ij >> 1, ij & 1
        first = pl.multiple_of(8 * j, 8)
        low = jnp.concatenate([phi_ref[8 * i + a, pl.ds(first, 16), 0:128] for a in range(11)], 0)
        high = jnp.concatenate([phi_ref[8 * i + a, pl.ds(first, 16), 128:256] for a in range(11)], 0)
        for m in range(8):
            window = pltpu.roll(low, (128 - 16 * m) % 128, 1) if m else low
            if m == 7:
                window = jnp.where(lane176 < 16, window, pltpu.roll(high, 16, 1))
            window = jnp.where(lane176 < 32, window, 0.0)
            part_h = window.astype(bf16).astype(f32)
            part_m = window - part_h
            left = (part_h + pltpu.roll(part_m, 32, 1) + pltpu.roll(part_h, 64, 1)).astype(bf16)
            stacks, slopes, sides = [], [], []
            for half in range(2):
                k = 2 * m + half
                ox = off_ref[0, i, j, k : k + 1]
                oy = off_ref[1, i, j, k : k + 1]
                oz = off_ref[2, i, j, k : k + 1]
                count = counts_ref[ij * 16 + k]
                weighted = jnp.where(lane < count, charge_ref[i, j, k : k + 1], 0.0)
                shifted = weights_at(oz, 32, 8 * half)
                for bag, value in ((stacks, spline(shifted)), (slopes, spline_slope(shifted))):
                    high_part, low_part = split2(value)
                    bag.append(jnp.concatenate([high_part, high_part, low_part, jnp.zeros((32, 128), bf16)], 0))
                sides.append((ox, oy, weighted))
            right = jnp.concatenate(stacks + slopes, 1)
            product = dot(left, right)
            for half in range(2):
                k = 2 * m + half
                ox, oy, weighted = sides[half]
                level = product[:, 128 * half : 128 * half + 128]
                rising = product[:, 256 + 128 * half : 384 + 128 * half]
                sx = weights_at(ox, 16, 0)
                sy = weights_at(oy, 16, 0)
                wx, gx = spline(sx), spline_slope(sx)
                wy, gy = spline(sy), spline_slope(sy)
                along = across = up = None
                for a in range(11):
                    piece = level[16 * a : 16 * a + 16]
                    rise = rising[16 * a : 16 * a + 16]
                    terms = (gx[a : a + 1] * piece, wx[a : a + 1] * piece, wx[a : a + 1] * rise)
                    if a == 0:
                        along, across, up = terms
                    else:
                        along, across, up = along + terms[0], across + terms[1], up + terms[2]
                force_x = jnp.sum(along * wy, axis=0, keepdims=True)
                force_y = jnp.sum(across * gy, axis=0, keepdims=True)
                force_z = jnp.sum(up * wy, axis=0, keepdims=True)
                out_ref[0, i, j, k : k + 1] = -weighted * force_x
                out_ref[1, i, j, k : k + 1] = -weighted * force_y
                out_ref[2, i, j, k : k + 1] = -weighted * force_z
        return 0

    lax.fori_loop(0, 4, column, 0)


def pair_scratch(cells, tiles):
    return (
        [
            pltpu.VMEM((tiles, 8, 128), f32),
            pltpu.VMEM((tiles, 48, 128), bf16),
            pltpu.VMEM((tiles, 16, 128), bf16),
            pltpu.VMEM((cells + 1, 128, 128), bf16),
            pltpu.VMEM(((cells + 1) * (128 // ROWS), 16, 128), f32),
        ]
        + [
            pltpu.VMEM((ROWS, TILES * 128), f32),
            pltpu.VMEM((ROWS, TILES * 128), bf16),
            pltpu.VMEM((ROWS, TILES * 128), bf16),
        ]
        * SLOTS
        + [pltpu.SMEM((16,), i32)]
        + [pltpu.SMEM((cells + 1,), i32)] * 3
    )


def pair_task(scratch, cells, levels, center, own_pos, own_count, own_level, emit):
    packed, features, sources, own_features, sums = scratch[:5]
    start, first_tile, groups_of, blocks_of = scratch[-4:]
    slots = [scratch[5 + 3 * e : 8 + 3 * e] for e in range(SLOTS)]
    blocks = 128 // ROWS
    lane = lax.broadcasted_iota(i32, (8, 128), 1)
    row = lax.broadcasted_iota(i32, (8, 128), 0)

    def add_level(level, carry, beads):
        end, current = carry
        start[level] = end
        for value, count in beads(level):
            within, tile = end & 127, end >> 7
            turned = pltpu.roll(value, within, 1)
            keep = lane < within
            current = jnp.where(keep, current, turned)
            packed[tile] = current
            end = end + count
            current = jnp.where((end >> 7) > tile, jnp.where(keep, turned, 0.0), current)
        packed[end >> 7] = current
        return end, current

    carry = (i32(0), jnp.zeros((8, 128), f32))
    for low, high, beads in levels:
        if high - low > 1:
            carry = lax.fori_loop(low, high, lambda n, c, beads=beads: add_level(n, c, beads), carry)
        else:
            carry = add_level(low, carry, beads)
    end, current = carry
    start[10] = end
    packed[end >> 7] = jnp.where(lane < (end & 127), current, 0.0)
    for e in range(1, TILES + 4):
        packed[(end >> 7) + e] = jnp.zeros((8, 128), f32)
    used = (end >> 7) + 1 + TILES
    middle = jnp.where(row < 2, 16.0, jnp.where(row == 2, center, 0.0))

    def near_step(step, _):
        for e in range(4):
            tile = 4 * step + e
            value = packed[tile] - middle
            norm = value[0:1] * value[0:1] + value[1:2] * value[1:2] + value[2:3] * value[2:3]
            vector = jnp.where(row < 3, value, jnp.where(row == 3, norm, jnp.where(row == 4, 1.0, 0.0)))
            h, m, l = split3(vector)
            features[tile] = jnp.concatenate([h, h, m, m, h, l], 0).astype(bf16)
            charge = value[3:4]
            vector = jnp.where(row < 3, value * charge, jnp.where(row == 3, charge, 0.0))
            h, m, l = split3(vector)
            sources[tile] = jnp.concatenate(
                [jnp.where(row < 4, h, pltpu.roll(m, 4, 0)), jnp.where(row < 4, l, 0.0)], 0
            ).astype(bf16)
        return 0

    lax.fori_loop(0, (used + 3) // 4, near_step, 0)

    def own_step(n, total):
        value = own_pos(n) - middle
        norm = value[0:1] * value[0:1] + value[1:2] * value[1:2] + value[2:3] * value[2:3]
        vector = jnp.where(
            row < 3,
            value * (2.0 / 64),
            jnp.where(row == 3, -1.0 / 64, jnp.where(row == 4, 1.0 - norm * (1.0 / 64), 0.0)),
        )
        h, m, l = split3(vector)
        stacked = jnp.concatenate([h, m, h, m, l, h, jnp.zeros((80, 128), f32)], 0)
        own_features[n] = jnp.transpose(stacked).astype(bf16)
        for e in range(blocks):
            sums[n * blocks + e] = jnp.zeros((16, 128), f32)
        level = own_level(n)
        begin, stop = start[level], start[level + 3]
        tile = begin >> 7
        groups = jnp.maximum((((stop + 127) >> 7) - tile + TILES - 1) // TILES, 1)
        rows = (own_count(n) + ROWS - 1) // ROWS
        first_tile[n], groups_of[n], blocks_of[n] = tile, groups, rows
        return total + groups * rows

    total = lax.fori_loop(0, cells, own_step, i32(0))
    own_features[cells] = jnp.zeros((128, 128), bf16)
    for e in range(blocks):
        sums[cells * blocks + e] = jnp.zeros((16, 128), f32)
    first_tile[cells], groups_of[cells], blocks_of[cells] = i32(0), i32(1), i32(1)
    for distance, high, low in slots:
        distance[...] = jnp.zeros((ROWS, TILES * 128), f32)
        high[...] = jnp.zeros((ROWS, TILES * 128), bf16)
        low[...] = jnp.zeros((ROWS, TILES * 128), bf16)

    def item(_, state):
        cell, block, group = state[:3]
        older, oldest = state[3 : 3 + 2 * SLOTS], state[3 + 2 * SLOTS :]
        added, shares, fresh, tags = [], [], [], []
        for e in range(SLOTS):
            distance, high, low = slots[e]
            tile = oldest[2 * e + 1]
            source = jnp.concatenate([sources[tile + s] for s in range(TILES)], 1)
            added.append(
                lax.dot_general(
                    jnp.concatenate([source, source], 1),
                    jnp.concatenate([high[...], low[...]], 1),
                    LAST,
                    preferred_element_type=f32,
                )
            )
            reach = distance[...]
            kept = jnp.maximum(reach, 0.0)
            strength = (kept * kept * kept) / (CAP - reach)
            shares.append(split2(strength))
            groups, rows = groups_of[cell], blocks_of[cell]
            tile = first_tile[cell] + group * TILES
            at = pl.multiple_of(block * ROWS, ROWS)
            left = own_features[cell, pl.ds(at, ROWS), 0:48]
            right = jnp.concatenate([features[tile + s] for s in range(TILES)], 1)
            fresh.append(dot(left, right))
            tags += [cell * blocks + block, tile]
            group = group + 1
            wrap = (group >= groups).astype(i32)
            group = group * (1 - wrap)
            block = block + wrap
            wrap = (block >= rows).astype(i32)
            block = block * (1 - wrap)
            cell = jnp.minimum(cell + wrap, cells)
        for e in range(SLOTS):
            distance, high, low = slots[e]
            where = oldest[2 * e]
            sums[where, :, 0:ROWS] = sums[where, :, 0:ROWS] + added[e]
            high[...], low[...] = shares[e]
            distance[...] = fresh[e]
        return (cell, block, group) + tuple(tags) + tuple(older)

    spare = (i32(cells * blocks), i32(0))
    lax.fori_loop(0, (total + SLOTS - 1) // SLOTS + 2, item, (i32(0),) * 3 + spare * (2 * SLOTS))

    def finish(n, _):
        parts = [sums[n * blocks + e, :, 0:ROWS] for e in range(blocks)]
        whole = jnp.concatenate(parts, 1) if blocks > 1 else parts[0]
        whole = whole[0:4] + whole[4:8] + whole[8:12]
        raw = own_pos(n)
        value = raw - middle
        emit(n, (value[0:3] * whole[3:4] - whole[0:3]) * (raw[3:4] * (1.0 / 64)), raw)
        return 0

    lax.fori_loop(0, cells, finish, 0)


def inner_pairs_kernel(part, near_ref, counts_ref, partners_ref, after_ref, out_ref, *scratch):
    lane = lax.broadcasted_iota(i32, (1, 128), 1)

    def count_at(x, y, k):
        return counts_ref[(x * 2 + y) * 16 + k]

    def place(n):
        return n >> 4, (n >> 3) & 1, 8 * part + (n & 7)

    def beads(level):
        at = 8 * part + level
        valid = ((at >= 1) & (at <= 16)).astype(i32)
        return [
            (near_ref[x, y, at], count_at(x, y, jnp.clip(at - 1, 0, 15)) * valid) for x in range(2) for y in range(2)
        ]

    def own_pos(n):
        x, y, k = place(n)
        return near_ref[x, y, k + 1]

    def emit(n, value, raw):
        x, y, k = place(n)
        count = count_at(x, y, k)
        partner = partners_ref[x, y, pl.ds(k, 1), :]
        other = jnp.take_along_axis(raw, jnp.broadcast_to(partner, (8, 128)), axis=1)
        both = (lane < count) & (partner < count)
        out_ref[x, y, n & 7, 0:3] = value + jnp.where(both, -0.1 * (raw[0:3] - other[0:3]), 0.0)

    pair_task(
        scratch, 32, [(0, 10, beads)], 64.0 * part + 40.0, own_pos, lambda n: count_at(*place(n)), lambda n: n & 7, emit
    )


def outer_pairs_kernel(near2_ref, own_msg_ref, below_ref, above_ref, first_ref, second_ref, out_ref,
                       near, counts, table, *scratch):
    dz = lax.axis_index("ga")
    row8 = lax.broadcasted_iota(i32, (8, 128), 0)
    for n, source in enumerate((below_ref, own_msg_ref, above_ref)):
        pltpu.sync_copy(source.at[0:8], counts.at[n])
    below_shift = jnp.where(row8 == 0, -16.0, 0.0)
    above_shift = jnp.where(row8 == 0, 16.0, 0.0)

    def level_step(level, _):
        for x in range(2):
            for y in range(4):
                near[x + 1, y, level] = near2_ref[x, y, level]
        for x, source, shift in ((0, below_ref, below_shift), (3, above_ref, above_shift)):
            for pair in range(2):
                at = pl.multiple_of(8 + 8 * (2 * level + pair), 8)
                got = source[pl.ds(at, 8)]
                near[x, 2 * pair, level] = jnp.where(row8 < 4, got, 0.0) + shift
                near[x, 2 * pair + 1, level] = jnp.where(row8 < 4, pltpu.roll(got, 4, 0), 0.0) + shift
        return 0

    lax.fori_loop(0, 18, level_step, 0)
    for x in range(4):
        which, along = ((0, 1), (1, 0), (1, 1), (2, 0))[x]
        for y in range(4):
            pair_row, across = ((2, 1), (0, 0), (0, 1), (4, 0))[y]
            base = 32 * along + 16 * across
            at = (x * 4 + y) * 18
            table[at] = jnp.where(dz == 1, counts[which, pair_row + 1, base + 15], 0.0).astype(i32)
            table[at + 17] = jnp.where(dz == 0, counts[which, pair_row + 1, base], 0.0).astype(i32)

            def copy_count(k, _, which=which, pair_row=pair_row, base=base, at=at):
                table[at + 1 + k] = counts[which, pair_row, base + k].astype(i32)
                return 0

            lax.fori_loop(0, 16, copy_count, 0)

    def count_at(x, y, level):
        return table[(x * 4 + y) * 18 + level]

    def task(number, _):
        part, j, i = number & 1, (number >> 1) & 1, number >> 2
        outside = [(3 * i, j), (3 * i, j + 1), (3 * i, j + 2), (1, 3 * j), (2, 3 * j)]
        within = [(1, 1), (1, 2), (2, 1), (2, 2)]

        def beads(level):
            return [(near[x, y, 8 * part + level], count_at(x, y, 8 * part + level)) for x, y in outside]

        def with_inner(level, use):
            return beads(level) + [
                (near[x, y, 8 * part + level], count_at(x, y, 8 * part + level) * use) for x, y in within
            ]

        def emit(n, value, raw):
            first, second = first_ref[i, j, n, 0:3], second_ref[i, j, n, 0:3]
            value = value + jnp.where(part == 0, first, second)
            for d in range(3):
                out_ref[d, i, j, pl.ds(8 * part + n, 1), :] = value[d : d + 1]

        pair_task(
            scratch,
            8,
            [(0, 1, lambda n: with_inner(n, 1 - part)), (1, 9, beads), (9, 10, lambda n: with_inner(n, part))],
            64.0 * part.astype(f32) + 40.0,
            lambda n: near[i + 1, j + 1, 8 * part + n + 1],
            lambda n: count_at(i + 1, j + 1, 8 * part + n + 1),
            lambda n: n,
            emit,
        )
        return 0

    lax.fori_loop(0, 8, task, 0)


def call(kernel, shapes, inputs, specs=None, scratch=(), flops=10**6, out_specs=None):
    single = not isinstance(shapes, (list, tuple)) or isinstance(shapes[0], int)
    shapes = [shapes] if single else shapes
    result = pl.pallas_call(
        kernel,
        out_shape=[jax.ShapeDtypeStruct(s, f32) for s in shapes],
        in_specs=specs or [VMEM] * len(inputs),
        out_specs=[VMEM] * len(shapes),
        scratch_shapes=list(scratch),
        cost_estimate=pl.CostEstimate(flops=flops, transcendentals=0, bytes_accessed=10**6),
        compiler_params=pltpu.CompilerParams(vmem_limit_bytes=40 << 20),
    )(*inputs)
    return result[0] if single else result


def move(value, axis, step):
    size = lax.axis_size(axis)
    return lax.ppermute(value, axis, [(n, n + step) for n in range(size) if 0 <= n + step < size])


def exchange(up, down, up2, down2, axis):
    return move(up, axis, 1), move(down, axis, -1), move(up2, axis, 2), move(down2, axis, -2)


def per_device(offsets, charge, counts, partners):
    z_op = jnp.asarray(np.stack([np.stack(halves(z_operator(part))) for part in range(2)]))
    fine_op, coarse_op, y_down, y_up = [jnp.asarray(m) for m in y_operators()]
    z_up = jnp.asarray(z_prolong())
    counts = counts.reshape(64)
    block = jnp.pad(counts.astype(f32)[None, :], ((0, 7), (0, 64)))
    near, rho, z_msg = call(
        spread_kernel,
        [(2, 2, 18, 8, 128), (19, 24, 256), (144, 128)],
        (offsets, charge, counts, block),
        [VMEM, VMEM, SMEM, VMEM],
    )
    z_got = lax.ppermute(z_msg, "ga", [(0, 1), (1, 0)])
    near1, full, restr, *y_msgs = call(
        along_z_kernel,
        [(2, 2, 18, 8, 128), (19, 24, 256), (19, 16, 128), (760, 128), (760, 128), (152, 128), (152, 128)],
        (near, rho, z_msg, z_got, z_op, y_down),
    )
    y_got = exchange(*y_msgs, "gy")
    inner = lambda part, near_in, after: call(
        lambda *refs: inner_pairs_kernel(part, *refs),
        (2, 2, 8, 8, 128),
        (near_in, counts, partners, after),
        [VMEM, SMEM, VMEM, ANY],
        pair_scratch(32, 40 + TILES + 10),
        flops=10**9,
    )
    first = inner(0, near, full)
    near2, fine2, _, *x_msgs = call(
        along_y_kernel,
        [(2, 4, 18, 8, 128), (19, 24, 256), (19, 16, 128), (824, 128), (824, 128), (48, 128), (48, 128)],
        (near1, full, restr, y_msgs[0], *y_got, fine_op, coarse_op, first),
        [VMEM] * 10 + [ANY],
    )
    x_got = exchange(*x_msgs, "gx")
    second = inner(1, near, fine2)
    phi = call(
        along_x_kernel,
        (19, 24, 256),
        (fine2, x_msgs[0], x_msgs[1], *x_got, y_up, z_up, second),
        [VMEM] * 9 + [ANY],
        [pltpu.VMEM((35, 24, 256), f32), pltpu.VMEM((19, 24, 256), f32), pltpu.VMEM((27, 16, 128), f32)],
    )
    short_force = call(
        outer_pairs_kernel,
        (3, 2, 2, 16, 128),
        (near2, x_msgs[0], x_got[0], x_got[1], first, second),
        None,
        [
            pltpu.VMEM((4, 4, 18, 8, 128), f32),
            pltpu.SMEM((3, 8, 128), f32),
            pltpu.SMEM((288,), i32),
        ]
        + pair_scratch(8, 56 + TILES + 10),
        flops=10**9,
    )
    long_force = call(
        gather_kernel, (3, 2, 2, 16, 128), (offsets, charge, counts, phi), [VMEM, VMEM, SMEM, VMEM]
    )
    return short_force, long_force


def solution(mesh):
    return jax.shard_map(
        per_device,
        mesh=mesh,
        in_specs=(
            P(None, "gx", "gy", "ga", None),
            P("gx", "gy", "ga", None),
            P("gx", "gy", "ga"),
            P("gx", "gy", "ga", None),
        ),
        out_specs=(P(None, "gx", "gy", "ga", None), P(None, "gx", "gy", "ga", None)),
        check_vma=False,
    )
```

time: 542 us -> 144 us (0.27)
  the two profiles are of different devices: /device:TPU:1 before, /device:TPU:115 now
where the time goes in v1:
time: 144 us; the launch traced here: 142 us
  Pallas kernels  110 us (76%)
  starting transfers between devices  24.8 us (17%)
  local copies, waits for them, and re-layouts  3.67 us (3%)
  waiting for transfers between devices  3.11 us (2%)
    pallas_call x8, Pallas kernels, call(): pl.pallas_call(kernel, out_shape=[jax.ShapeDtypeStruct(s, f32) for s in s...  110 us
    ppermute x8, starting transfers between devices, move(): lax.ppermute(value, axis, [(n, n + step) for n in range(size) if 0 <= n +...  24.6 us
    ppermute x1, waiting for transfers between devices, per_device(): z_got = lax.ppermute(z_msg, 'ga', [(0, 1), (1, 0)])  3.08 us
  transfers between devices with their start and end apart: 9, of which 1 were waited for; matrix products, arithmetic and copies ran while one was open for 0% of the time, Pallas kernels for 27%

profile of v1, /device:TPU:115, one launch (start us, length us, event | category | flops | bytes accessed | tf_op | source)
XLA Modules:
  0.0 142.1 jit_solution(17031380276792158463)
XLA Ops:
  0.6 0.8 reshape.18.counts_ref.refs_1_
  1.5 0.1 convert_element_type.16
  1.6 0.9 copy-done.1
  2.5 0.8 copy-done.3
  3.2 4.1 %shard_map.113 = (f32[2,2,18,8,128]{4,3,2,1,0:T(8,128)S(1)}, f32[19,24,256]{2,1,0:T(8,128)S(1)}, f32[144,128]{1,0:T(8,128)S(1)}) custom-call(f32[3,2,2,16,128]{4,3,2,1,0:T(8,128)S(1)} %copy-done.1, f32[2,2,16,128]{3,2,1,0:T(8,128)S(1)} %copy-done.3, s32[64]{0:T(128)S(1)} %reshape.18.counts_ref.refs_1_, f32[8,128]{1,0:T(8,128)S(1)} %pad.4.block_ref), custom_call_target="tpu_custom_call" | custom-call | flops 1000000 | bytes 1000000 | tf_op jit(solution)/shard_map/pallas_call | solution.py:754
  7.4 0.0 copy-start.9
  7.4 0.2 collective-permute-start
  7.6 3.1 %collective-permute-done.got_ref = f32[144,128]{1,0:T(8,128)S(1)} collective-permute-done((f32[144,128]{1,0:T(8,128)S(1)}, f32[144,128]{1,0:T(8,128)S(1)}, u32[]{:S(2)}, u32[]{:S(2)}) %collective-permute-start) | collective-permute-done | bytes 73760 | tf_op jit(solution)/shard_map/ppermute | solution.py:787
  10.7 1.0 copy-done
  11.7 1.1 shard_map.114
  12.8 2.2 %collective-permute-start.2 = (f32[760,128]{1,0:T(8,128)S(1)}, f32[760,128]{1,0:T(8,128)S(1)}, u32[]{:S(2)}, u32[]{:S(2)}) collective-permute-start(f32[760,128]{1,0:T(8,128)S(1)} %get-tuple-element.25), channel_id=1, source_target_pairs={{2,0},{4,2},{6,4},{8,6},{10,8},{12,10},{14,12},{3,1},{5,3},{7,5},{... | collective-permute-start | bytes 1167368 | tf_op jit(solution)/shard_map/ppermute | solution.py:768
  15.0 5.5 %collective-permute-start.1 = (f32[760,128]{1,0:T(8,128)S(1)}, f32[760,128]{1,0:T(8,128)S(1)}, u32[]{:S(2)}, u32[]{:S(2)}) collective-permute-start(f32[760,128]{1,0:T(8,128)S(1)} %get-tuple-element.24.up_own_ref), channel_id=1, source_target_pairs={{0,2},{2,4},{4,6},{6,8},{8,10},{10,12},{12,14},{1,3},{3,5},{5,7},{... | collective-permute-start | bytes 1167368 | tf_op jit(solution)/shard_map/ppermute | solution.py:768
  20.5 3.1 %collective-permute-start.3 = (f32[152,128]{1,0:T(8,128)S(1)}, f32[152,128]{1,0:T(8,128)S(1)}, u32[]{:S(2)}, u32[]{:S(2)}) collective-permute-start(f32[152,128]{1,0:T(8,128)S(1)} %get-tuple-element.26), channel_id=1, source_target_pairs={{0,4},{2,6},{4,8},{6,10},{8,12},{10,14},{1,5},{3,7},{5,9},{7,11},{... | collective-permute-start | bytes 233480 | tf_op jit(solution)/shard_map/ppermute | solution.py:768
  23.6 2.2 %collective-permute-start.4 = (f32[152,128]{1,0:T(8,128)S(1)}, f32[152,128]{1,0:T(8,128)S(1)}, u32[]{:S(2)}, u32[]{:S(2)}) collective-permute-start(f32[152,128]{1,0:T(8,128)S(1)} %get-tuple-element.27), channel_id=1, source_target_pairs={{4,0},{6,2},{8,4},{10,6},{12,8},{14,10},{5,1},{7,3},{9,5},{11,7},{... | collective-permute-start | bytes 233480 | tf_op jit(solution)/shard_map/ppermute | solution.py:768
  25.8 18.0 %shard_map.115.after_ref.first_ref = f32[2,2,8,8,128]{4,3,2,1,0:T(8,128)S(1)} custom-call(f32[2,2,18,8,128]{4,3,2,1,0:T(8,128)S(1)} %get-tuple-element.18.near_ref.refs_0_, s32[64]{0:T(128)S(1)} %reshape.18.counts_ref.refs_1_, s32[2,2,16,128]{3,2,1,0:T(8,128)S(1)} %copy-done.10, f32[19,24,256]{2,1,0:T(8,128)S(1)} %get-tuple-element.22.refs_3_.full_ref), custom_call_target="tpu_custom_call" | custom-call | flops 1000000000 | bytes 1000000 | tf_op jit(solution)/shard_map/pallas_call | solution.py:754
  43.9 3.6 %shard_map.116 = (f32[2,4,18,8,128]{4,3,2,1,0:T(8,128)S(1)}, f32[19,24,256]{2,1,0:T(8,128)S(1)}, f32[19,16,128]{2,1,0:T(8,128)}, f32[824,128]{1,0:T(8,128)S(1)},...) custom-call(f32[2,2,18,8,128]{4,3,2,1,0:T(8,128)S(1)} %get-tuple-element.21.near1_ref, ...), custom_call_target="tpu_custom_call" | custom-call | flops 1000000 | bytes 1000000 | tf_op jit(solution)/shard_map/pallas_call | solution.py:754
  47.5 3.1 %collective-permute-start.6 = (f32[824,128]{1,0:T(8,128)S(1)}, f32[824,128]{1,0:T(8,128)S(1)}, u32[]{:S(2)}, u32[]{:S(2)}) collective-permute-start(f32[824,128]{1,0:T(8,128)S(1)} %get-tuple-element.30.dn_own_ref), channel_id=1, source_target_pairs={{16,0},{32,16},{48,32},{64,48},{80,64},{96,80},{112,96},{17,1},{33... | collective-permute-start | bytes 1265672 | tf_op jit(solution)/shard_map/ppermute | solution.py:768
  50.6 2.5 %collective-permute-start.5 = (f32[824,128]{1,0:T(8,128)S(1)}, f32[824,128]{1,0:T(8,128)S(1)}, u32[]{:S(2)}, u32[]{:S(2)}) collective-permute-start(f32[824,128]{1,0:T(8,128)S(1)} %get-tuple-element.29.own_msg_ref.up_own_ref), channel_id=1, source_target_pairs={{0,16},{16,32},{32,48},{48,64},{64,80},{80,96},{96,112},{1,17},{17... | collective-permute-start | bytes 1265672 | tf_op jit(solution)/shard_map/ppermute | solution.py:768
  53.1 1.9 %collective-permute-start.7 = (f32[48,128]{1,0:T(8,128)S(1)}, f32[48,128]{1,0:T(8,128)S(1)}, u32[]{:S(2)}, u32[]{:S(2)}) collective-permute-start(f32[48,128]{1,0:T(8,128)S(1)} %get-tuple-element.32), channel_id=1, source_target_pairs={{0,32},{16,48},{32,64},{48,80},{64,96},{80,112},{1,33},{17,49},{33... | collective-permute-start | bytes 73736 | tf_op jit(solution)/shard_map/ppermute | solution.py:768
  55.0 4.1 %collective-permute-start.8 = (f32[48,128]{1,0:T(8,128)S(1)}, f32[48,128]{1,0:T(8,128)S(1)}, u32[]{:S(2)}, u32[]{:S(2)}) collective-permute-start(f32[48,128]{1,0:T(8,128)S(1)} %get-tuple-element.33), channel_id=1, source_target_pairs={{32,0},{48,16},{64,32},{80,48},{96,64},{112,80},{33,1},{49,17},{65... | collective-permute-start | bytes 73736 | tf_op jit(solution)/shard_map/ppermute | solution.py:768
  59.1 19.8 %shard_map.117.second_ref.after_ref = f32[2,2,8,8,128]{4,3,2,1,0:T(8,128)S(1)} custom-call(f32[2,2,18,8,128]{4,3,2,1,0:T(8,128)S(1)} %get-tuple-element.18.near_ref.refs_0_, s32[64]{0:T(128)S(1)} %reshape.18.counts_ref.refs_1_, s32[2,2,16,128]{3,2,1,0:T(8,128)S(1)} %copy-done.10, f32[19,24,256]{2,1,0:T(8,128)S(1)} %get-tuple-element.31.refs_3_.fine2_ref), custom_call_target="tpu_custom_call" | custom-call | flops 1000000000 | bytes 1000000 | tf_op jit(solution)/shard_map/pallas_call | solution.py:754
  79.0 1.6 %shard_map.119.phi_ref = f32[19,24,256]{2,1,0:T(8,128)S(1)} custom-call(f32[19,24,256]{2,1,0:T(8,128)S(1)} %get-tuple-element.31.refs_3_.fine2_ref, f32[824,128]{1,0:T(8,128)S(1)} %get-tuple-element.29.own_msg_ref.up_own_ref, f32[824,128]{1,0:T(8,128)S(1)} %get-tuple-element.30.dn_own_ref, f32[824,128]{1,0:T(8,128)S(1)} %collective-permute-done.5.below_ref, ...), custom_call_target="tpu_custom_call" | custom-call | flops 1000000 | bytes 1000000 | tf_op jit(solution)/shard_map/pallas_call | solution.py:754
  80.6 5.9 %shard_map.120 = f32[3,2,2,16,128]{4,3,2,1,0:T(8,128)} custom-call(f32[3,2,2,16,128]{4,3,2,1,0:T(8,128)S(1)} %copy-done.2, f32[2,2,16,128]{3,2,1,0:T(8,128)S(1)} %copy-done.4, s32[64]{0:T(128)S(1)} %reshape.18.counts_ref.refs_1_, f32[19,24,256]{2,1,0:T(8,128)S(1)} %shard_map.119.phi_ref), custom_call_target="tpu_custom_call" | custom-call | flops 1000000 | bytes 1000000 | tf_op jit(solution)/shard_map/pallas_call | solution.py:754
  86.5 55.5 %shard_map.118 = f32[3,2,2,16,128]{4,3,2,1,0:T(8,128)} custom-call(f32[2,4,18,8,128]{4,3,2,1,0:T(8,128)S(1)} %get-tuple-element.28.near2_ref, f32[824,128]{1,0:T(8,128)S(1)} %get-tuple-element.29.own_msg_ref.up_own_ref, f32[824,128]{1,0:T(8,128)S(1)} %collective-permute-done.5.below_ref, f32[824,128]{1,0:T(8,128)S(1)} %collective-permute-done.6.above_ref, ...), custom_call_target="tpu_custom_call" | custom-call | flops 1000000000 | bytes 1000000 | tf_op jit(solution)/shard_map/pallas_call | solution.py:754
  (30 shorter events, 0.1 us)
Async XLA Ops:
  0.6 0.8 copy-start.11
  1.6 0.9 copy-start.1
  2.5 0.8 copy-start.3
  7.4 3.3 %copy-start.9 = (bf16[16,72]{1,0:T(8,128)(2,1)S(1)}, bf16[16,72]{1,0:T(8,128)(2,1)}, u32[]{:S(2)}) copy-start(bf16[16,72]{1,0:T(8,128)(2,1)} %constant.18.clone.down_ref) | copy-start | bytes 6916
  7.4 3.3 %collective-permute-start = (f32[144,128]{1,0:T(8,128)S(1)}, f32[144,128]{1,0:T(8,128)S(1)}, u32[]{:S(2)}, u32[]{:S(2)}) collective-permute-start(f32[144,128]{1,0:T(8,128)S(1)} %get-tuple-element.20.own_msg_ref), channel_id=1, source_target_pairs={{0,1},{1,0},{2,3},{3,2},{4,5},{5,4},{6,7},{7,6},{8,9},{9,8},{10,11... | collective-permute-start | bytes 221192 | tf_op jit(solution)/shard_map/ppermute | solution.py:787
  10.7 1.0 copy-start
  11.7 14.1 %copy-start.10 = (s32[2,2,16,128]{3,2,1,0:T(8,128)S(1)}, s32[2,2,16,128]{3,2,1,0:T(8,128)}, u32[]{:S(2)}) copy-start(s32[2,2,16,128]{3,2,1,0:T(8,128)} %refs_2_.3) | copy-start | bytes 98308
  12.8 31.1 %collective-permute-start.2 = (f32[760,128]{1,0:T(8,128)S(1)}, f32[760,128]{1,0:T(8,128)S(1)}, u32[]{:S(2)}, u32[]{:S(2)}) collective-permute-start(f32[760,128]{1,0:T(8,128)S(1)} %get-tuple-element.25), channel_id=1, source_target_pairs={{2,0},{4,2},{6,4},{8,6},{10,8},{12,10},{14,12},{3,1},{5,3},{7,5},{... | collective-permute-start | bytes 1167368 | tf_op jit(solution)/shard_map/ppermute | solution.py:768
  15.0 28.9 %collective-permute-start.1 = (f32[760,128]{1,0:T(8,128)S(1)}, f32[760,128]{1,0:T(8,128)S(1)}, u32[]{:S(2)}, u32[]{:S(2)}) collective-permute-start(f32[760,128]{1,0:T(8,128)S(1)} %get-tuple-element.24.up_own_ref), channel_id=1, source_target_pairs={{0,2},{2,4},{4,6},{6,8},{8,10},{10,12},{12,14},{1,3},{3,5},{5,7},{... | collective-permute-start | bytes 1167368 | tf_op jit(solution)/shard_map/ppermute | solution.py:768
  20.5 23.4 %collective-permute-start.3 = (f32[152,128]{1,0:T(8,128)S(1)}, f32[152,128]{1,0:T(8,128)S(1)}, u32[]{:S(2)}, u32[]{:S(2)}) collective-permute-start(f32[152,128]{1,0:T(8,128)S(1)} %get-tuple-element.26), channel_id=1, source_target_pairs={{0,4},{2,6},{4,8},{6,10},{8,12},{10,14},{1,5},{3,7},{5,9},{7,11},{... | collective-permute-start | bytes 233480 | tf_op jit(solution)/shard_map/ppermute | solution.py:768
  23.6 20.3 %collective-permute-start.4 = (f32[152,128]{1,0:T(8,128)S(1)}, f32[152,128]{1,0:T(8,128)S(1)}, u32[]{:S(2)}, u32[]{:S(2)}) collective-permute-start(f32[152,128]{1,0:T(8,128)S(1)} %get-tuple-element.27), channel_id=1, source_target_pairs={{4,0},{6,2},{8,4},{10,6},{12,8},{14,10},{5,1},{7,3},{9,5},{11,7},{... | collective-permute-start | bytes 233480 | tf_op jit(solution)/shard_map/ppermute | solution.py:768
  25.8 18.1 %copy-start.6 = (bf16[24,168]{1,0:T(8,128)(2,1)S(1)}, bf16[24,168]{1,0:T(8,128)(2,1)}, u32[]{:S(2)}) copy-start(bf16[24,168]{1,0:T(8,128)(2,1)} %constant.16.clone.fine_ref) | copy-start | bytes 24196
  25.8 18.1 %copy-start.7 = (bf16[16,192]{1,0:T(8,128)(2,1)S(1)}, bf16[16,192]{1,0:T(8,128)(2,1)}, u32[]{:S(2)}) copy-start(bf16[16,192]{1,0:T(8,128)(2,1)} %constant.17.clone.coarse_ref) | copy-start | bytes 18436
  47.5 31.5 %collective-permute-start.6 = (f32[824,128]{1,0:T(8,128)S(1)}, f32[824,128]{1,0:T(8,128)S(1)}, u32[]{:S(2)}, u32[]{:S(2)}) collective-permute-start(f32[824,128]{1,0:T(8,128)S(1)} %get-tuple-element.30.dn_own_ref), channel_id=1, source_target_pairs={{16,0},{32,16},{48,32},{64,48},{80,64},{96,80},{112,96},{17,1},{33... | collective-permute-start | bytes 1265672 | tf_op jit(solution)/shard_map/ppermute | solution.py:768
  50.6 28.4 %collective-permute-start.5 = (f32[824,128]{1,0:T(8,128)S(1)}, f32[824,128]{1,0:T(8,128)S(1)}, u32[]{:S(2)}, u32[]{:S(2)}) collective-permute-start(f32[824,128]{1,0:T(8,128)S(1)} %get-tuple-element.29.own_msg_ref.up_own_ref), channel_id=1, source_target_pairs={{0,16},{16,32},{32,48},{48,64},{64,80},{80,96},{96,112},{1,17},{17... | collective-permute-start | bytes 1265672 | tf_op jit(solution)/shard_map/ppermute | solution.py:768
  53.1 25.9 %collective-permute-start.7 = (f32[48,128]{1,0:T(8,128)S(1)}, f32[48,128]{1,0:T(8,128)S(1)}, u32[]{:S(2)}, u32[]{:S(2)}) collective-permute-start(f32[48,128]{1,0:T(8,128)S(1)} %get-tuple-element.32), channel_id=1, source_target_pairs={{0,32},{16,48},{32,64},{48,80},{64,96},{80,112},{1,33},{17,49},{33... | collective-permute-start | bytes 73736 | tf_op jit(solution)/shard_map/ppermute | solution.py:768
  55.0 24.0 %collective-permute-start.8 = (f32[48,128]{1,0:T(8,128)S(1)}, f32[48,128]{1,0:T(8,128)S(1)}, u32[]{:S(2)}, u32[]{:S(2)}) collective-permute-start(f32[48,128]{1,0:T(8,128)S(1)} %get-tuple-element.33), channel_id=1, source_target_pairs={{32,0},{48,16},{64,32},{80,48},{96,64},{112,80},{33,1},{49,17},{65... | collective-permute-start | bytes 73736 | tf_op jit(solution)/shard_map/ppermute | solution.py:768
  59.1 19.9 %copy-start.5 = (bf16[128,256]{1,0:T(8,128)(2,1)S(1)}, bf16[128,256]{1,0:T(8,128)(2,1)}, u32[]{:S(2)}) copy-start(bf16[128,256]{1,0:T(8,128)(2,1)} %constant.20.clone.up_z_ref) | copy-start | bytes 196612
  59.1 19.9 %copy-start.8 = (bf16[24,48]{1,0:T(8,128)(2,1)S(1)}, bf16[24,48]{1,0:T(8,128)(2,1)}, u32[]{:S(2)}) copy-start(bf16[24,48]{1,0:T(8,128)(2,1)} %constant.19.clone.up_y_ref) | copy-start | bytes 6916
  78.9 1.7 %copy-start.2 = (f32[3,2,2,16,128]{4,3,2,1,0:T(8,128)S(1)}, f32[3,2,2,16,128]{4,3,2,1,0:T(8,128)}, u32[]{:S(2)}) copy-start(f32[3,2,2,16,128]{4,3,2,1,0:T(8,128)} %off_ref.3) | copy-start | bytes 294916
  78.9 1.7 %copy-start.4 = (f32[2,2,16,128]{3,2,1,0:T(8,128)S(1)}, f32[2,2,16,128]{3,2,1,0:T(8,128)}, u32[]{:S(2)}) copy-start(f32[2,2,16,128]{3,2,1,0:T(8,128)} %charge_ref.3) | copy-start | bytes 98308
